TPU v7x, 256 devices: a whole 4x4x8 slice. The times are simulated.
256 devices in a mesh: kern: 2 (over core), ty: 16 (over x, z_hi), tx: 8 (over z_lo, y).
Axes of the slice: x: 4, y: 4, z: 8 (z_hi: 4, z_lo: 2; z = z_hi * 2 + z_lo), core: 2. Of those that a mesh axis runs over, the one named last changes fastest.
Arguments:
- mask: float32 [4096, 2048], P('ty', 'tx'), may hold values from -1 to 1
- target: int32 [4096, 2048], P('ty', 'tx'), may hold values 0 or 1
- spectra: float32 [2, 24, 128, 128], P(None, 'kern'), may hold values from -4.5 to 4.5
Outputs:
- resist: float32 [4096, 2048], P('ty', 'tx')
- mask_grad: float32 [4096, 2048], P('ty', 'tx')
All inputs are finite; a program needn't handle non-finite values. No bound on the sum of `target` on one device may be relied on, other than what follows from the above.
Results may differ from a plain program's by a relative error of at most 0.0003.
Values sent between devices are 32-bit elements; how exact they have to be, the bound alone decides.
A program may use at most 64 MiB of HBM per device.

v0:
```python
import math

import jax
import jax.numpy as jnp
import numpy as np
from jax import lax
from jax.experimental import pallas as pl
from jax.experimental.pallas import tpu as pltpu
from jax.sharding import PartitionSpec as P

TILE = 256
HALO = 64
BAND = 128
WINDOW = TILE + 2 * HALO
HALF = TILE // 2
STEEP = 8.0
LEVEL = 1.0
UNROLL = 2
SCALE = 1.0 / (WINDOW * WINDOW)
MESH = pl.DeviceIdType.MESH
F32 = jnp.float32
BF16 = jnp.bfloat16


def halves(table):
    table = np.asarray(table, np.float32)
    hi = table.astype(BF16)
    lo = (table - hi.astype(np.float32)).astype(BF16)
    return hi, lo


def make_tables():
    freq = np.arange(BAND) - BAND // 2
    order = np.concatenate(
        [np.arange(TILE) + HALO, np.arange(HALO), np.arange(HALO) + HALO + TILE]
    )
    angle = np.mod(order[:, None] * freq[None, :], WINDOW).astype(np.float64) * (2.0 * math.pi / WINDOW)
    c, s = np.cos(angle), np.sin(angle)
    by_place = np.concatenate([c, -s, s, c], 1)
    by_freq = np.block([[c.T, s.T], [-s.T, c.T]])
    return np.stack(halves(by_place)), np.stack(halves(by_freq))


def split(x):
    hi = x.astype(BF16)
    return hi, (x - hi.astype(F32)).astype(BF16)


def dot(a, b):
    return jnp.dot(a, b, preferred_element_type=F32)


def rows_by_table(x, table):
    hi, lo = split(x)
    t_hi, t_lo = table
    left = jnp.concatenate([hi, lo, hi], axis=1)
    return dot(left, jnp.concatenate([t_hi, t_hi, t_lo], axis=0))


def table_by_rows(table, hi, lo):
    t_hi, t_lo = table
    left = jnp.concatenate([t_hi, t_hi, t_lo], axis=1)
    return dot(left, jnp.concatenate([hi, lo, hi], axis=0))


def fold(a, b):
    left_lanes = lax.broadcasted_iota(jnp.int32, a.shape, 1) < HALO
    first = jnp.where(left_lanes, a, pltpu.roll(b, HALO, 1))
    second = jnp.where(left_lanes, pltpu.roll(a, HALO, 1), b)
    return first, second


def body(
    mask_h, target_h, spec_h, place_h, freq_h,
    resist_h, grad_h,
    mask_v, target_v, spec_v, place_v, freq_v,
    send_side, send_diag, got_v, got_side, got_diag,
    acc_half, a_stack, f_part, f_got, r_stack, field, inten, inten_got, weight, resist_v,
    c_stack, w_part, w_got, g_v, g_side, g_diag, gg_v, gg_side, gg_diag, out_half,
    load_sem, store_sem, h_send, h_recv, p_send, p_recv, g_send, g_recv,
):
    kern, ty, tx = lax.axis_index("kern"), lax.axis_index("ty"), lax.axis_index("tx")
    n_ty, n_tx = lax.axis_size("ty"), lax.axis_size("tx")
    other = 1 - kern
    vt = ty - 1 + 2 * kern
    has_v = jnp.logical_and(vt >= 0, vt < n_ty)
    has_l, has_r = tx > 0, tx < n_tx - 1
    has_dl, has_dr = jnp.logical_and(has_v, has_l), jnp.logical_and(has_v, has_r)
    partner = (other, ty, tx)
    vertical = (other, vt, tx)
    left, right = (kern, ty, tx - 1), (kern, ty, tx + 1)
    diag_l, diag_r = (other, vt, tx - 1), (other, vt, tx + 1)
    peers = [(has_v, vertical), (has_l, left), (has_r, right), (has_dl, diag_l), (has_dr, diag_r)]

    barrier = pltpu.get_barrier_semaphore()
    pl.semaphore_signal(barrier, inc=1, device_id=partner, device_id_type=MESH)
    for has, peer in peers:

        @pl.when(has)
        def _(peer=peer):
            pl.semaphore_signal(barrier, inc=1, device_id=peer, device_id_type=MESH)

    loads = [
        (mask_h, mask_v), (place_h, place_v), (freq_h, freq_v), (spec_h, spec_v), (target_h, target_v),
    ]
    loads = [pltpu.make_async_copy(a, b, load_sem.at[i]) for i, (a, b) in enumerate(loads)]
    for load in loads:
        load.start()
    l_mask, l_place, l_freq, l_spec, l_target = loads

    def place(rows, lanes):
        return place_v[0, rows, lanes], place_v[1, rows, lanes]

    def inverse_lanes(part):
        both = jnp.concatenate([freq_v[part, :, :TILE], freq_v[part, :, WINDOW : WINDOW + TILE]], axis=1)
        return both

    def block_of(first, second, axis):
        return tuple(jnp.concatenate([a, b], axis=axis) for a, b in zip(first, second))

    inner, direct, turned = slice(0, TILE), slice(0, TILE), slice(TILE, 2 * TILE)
    edges = slice(TILE, WINDOW)

    a_stack[...] = jnp.zeros(a_stack.shape, BF16)
    for has, bufs in (
        (has_v, (got_v, gg_v)),
        (has_l, (got_side.at[0], gg_side.at[0])),
        (has_r, (got_side.at[1], gg_side.at[1])),
        (has_dl, (got_diag.at[0], gg_diag.at[0])),
        (has_dr, (got_diag.at[1], gg_diag.at[1])),
    ):

        @pl.when(jnp.logical_not(has))
        def _(bufs=bufs):
            for buf in bufs:
                buf[...] = jnp.zeros(buf.shape, F32)

    half_at = pl.multiple_of(kern * HALF, HALF)
    edge_at = pl.multiple_of(kern * (TILE - HALO), HALO)
    l_mask.wait()
    mask_half = mask_v[pl.ds(half_at, HALF), :]
    mask_edge = mask_v[pl.ds(edge_at, HALO), :]

    def side_lanes(x):
        lanes = lax.broadcasted_iota(jnp.int32, (x.shape[0], 128), 1) < HALO
        return jnp.where(lanes, x[:, :128], x[:, 128:])

    sides = side_lanes(mask_half)
    first, second = fold(sides[:64], sides[64:])
    send_side[0] = first
    send_side[1] = second
    corners = side_lanes(mask_edge)
    first, second = fold(corners[:32], corners[32:])
    send_diag[0] = first
    send_diag[1] = second

    pl.semaphore_wait(barrier, 1 + sum(has.astype(jnp.int32) for has, _ in peers))

    def remote(src, dst, send, recv, at, peer):
        return pltpu.make_async_remote_copy(
            src_ref=src, dst_ref=dst, send_sem=send.at[at], recv_sem=recv.at[at],
            device_id=peer, device_id_type=MESH,
        )

    def exchange(src_v, src_side, src_diag, dst_v, dst_side, dst_diag, send, recv):
        return [
            (has_v, has_v, remote(src_v, dst_v, send, recv, 0, vertical)),
            (has_l, has_r, remote(src_side.at[0], dst_side.at[1], send, recv, 1, left)),
            (has_r, has_l, remote(src_side.at[1], dst_side.at[0], send, recv, 2, right)),
            (has_dl, has_dr, remote(src_diag.at[0], dst_diag.at[1], send, recv, 3, diag_l)),
            (has_dr, has_dl, remote(src_diag.at[1], dst_diag.at[0], send, recv, 4, diag_r)),
        ]

    def each(copies, which, act):
        for entry in copies:

            @pl.when(entry[which])
            def _(copy=entry[2]):
                act(copy)

    halo = exchange(
        mask_v.at[pl.ds(edge_at, HALO)], send_side, send_diag, got_v, got_side, got_diag,
        h_send, h_recv,
    )
    each(halo, 0, lambda c: c.start())

    l_place.wait()
    own = place(inner, direct)
    acc_half[...] = rows_by_table(mask_half, own)
    l_freq.wait()
    each(halo, 1, lambda c: c.wait_recv())

    top, bottom = fold(got_side[0], got_side[1])
    side_part = rows_by_table(jnp.concatenate([top, bottom], axis=0), place(edges, direct))
    half_hi, half_lo = split(acc_half[...] + side_part)
    top, bottom = fold(got_diag[0], got_diag[1])
    strip = rows_by_table(got_v[...], own)
    strip = strip + rows_by_table(jnp.concatenate([top, bottom], axis=0), place(edges, direct))
    strip_hi, strip_lo = split(strip)
    edge_rows = pl.ds(pl.multiple_of(HALF + kern * HALO, HALO), HALO)
    for part, (main, edge) in enumerate(((half_hi, strip_hi), (half_lo, strip_lo))):
        a_stack[part, pl.ds(0, HALF), :] = main
        a_stack[part, edge_rows, :] = edge
    half_lanes = pl.ds(half_at, HALF)
    own_y = []
    for part in range(2):
        cos = [freq_v[part, pl.ds(0, BAND), half_lanes], freq_v[part, :BAND, TILE:WINDOW]]
        sin_lanes = pl.ds(pl.multiple_of(WINDOW + half_at, HALF), HALF)
        sin = [freq_v[part, pl.ds(0, BAND), sin_lanes], freq_v[part, :BAND, WINDOW + TILE :]]
        own_y.append(jnp.concatenate([jnp.concatenate(cos, axis=1), jnp.concatenate(sin, axis=1)], axis=0))
    full = table_by_rows(own_y, a_stack[0], a_stack[1])
    f_part[:, :BAND] = full[:BAND, :BAND] + full[BAND:, BAND:]
    f_part[:, BAND:] = full[:BAND, BAND:] - full[BAND:, :BAND]
    f_copy = remote(f_part, f_got, p_send, p_recv, 0, partner)
    f_copy.start()
    l_spec.wait()
    f_copy.wait_recv()
    w_part[...] = (f_part[...] + f_got[...]) * SCALE

    kernels = spec_v.shape[1]

    def loop(step):
        def several(i, carry):
            for j in range(UNROLL):
                step(i * UNROLL + j)
            return carry

        lax.fori_loop(0, kernels // UNROLL, several, 0)

    def to_columns(k):
        f_re, f_im = w_part[:, :BAND], w_part[:, BAND:]
        h_re, h_im = spec_v[0, k], spec_v[1, k]
        prod = jnp.concatenate([f_re * h_re - f_im * h_im, f_re * h_im + f_im * h_re], axis=1)
        hi, lo = split(rows_by_table(prod, (inverse_lanes(0), inverse_lanes(1))))
        r_stack[k, pl.ds(0, 128), :] = hi[:, :TILE]
        r_stack[k, pl.ds(128, 128), :] = hi[:, TILE:]
        r_stack[k, pl.ds(256, 128), :] = lo[:, :TILE]
        r_stack[k, pl.ds(384, 128), :] = lo[:, TILE:]

    loop(to_columns)

    i_copies = []
    for b in range(2):
        inten[b] = jnp.zeros((HALF, TILE), F32)

        def to_rows(k, b=b):
            at = slice(b * HALF, (b + 1) * HALF)
            hi, lo = r_stack[k, pl.ds(0, TILE), :], r_stack[k, pl.ds(TILE, TILE), :]
            value = table_by_rows(block_of(place(at, direct), place(at, turned), 0), hi, lo)
            field[b, k] = value
            re, im = value[:HALF], value[HALF:]
            inten[b] += re * re + im * im

        loop(to_rows)
        copy = remote(inten.at[b], inten_got.at[b], p_send, p_recv, 1 + b, partner)
        copy.start()
        i_copies.append(copy)

    l_target.wait()
    stores = []
    for b in range(2):
        i_copies[b].wait_recv()
        rows = pl.ds(b * HALF, HALF)
        resist = jax.nn.sigmoid(STEEP * (inten[b] + inten_got[b] - LEVEL))
        goal = target_v[rows, :].astype(F32)
        resist_v[rows, :] = resist
        weight[...] = 2.0 * (resist - goal) * STEEP * resist * (1.0 - resist)
        store = pltpu.make_async_copy(resist_v.at[rows], resist_h.at[rows], store_sem.at[b])
        store.start()
        stores.append(store)

        def back_columns(k, b=b):
            w = weight[...]
            load = jnp.concatenate([w * field[b, k, pl.ds(0, HALF), :], w * field[b, k, pl.ds(HALF, HALF), :]], axis=1)
            hi, lo = split(rows_by_table(load, block_of(place(inner, direct), place(inner, turned), 0)))
            c_stack[k, pl.ds(b * HALF, HALF), :] = hi
            c_stack[k, pl.ds(TILE + b * HALF, HALF), :] = lo

        loop(back_columns)

    f_copy.wait_send()
    f_part[...] = jnp.zeros((BAND, 2 * BAND), F32)

    def back_rows(k):
        hi, lo = c_stack[k, pl.ds(0, TILE), :], c_stack[k, pl.ds(TILE, TILE), :]
        value = table_by_rows([jnp.concatenate([freq_v[part, :BAND, :TILE], freq_v[part, :BAND, WINDOW : WINDOW + TILE]], axis=0) for part in range(2)], hi, lo)
        s_re = value[:BAND, :BAND] + value[BAND:, BAND:]
        s_im = value[:BAND, BAND:] - value[BAND:, :BAND]
        h_re, h_im = spec_v[0, k], spec_v[1, k]
        f_part[:, :BAND] += h_re * s_re + h_im * s_im
        f_part[:, BAND:] += h_re * s_im - h_im * s_re

    loop(back_rows)
    w_copy = remote(f_part, w_got, p_send, p_recv, 3, partner)
    w_copy.start()
    w_copy.wait_recv()

    lifted = rows_by_table((f_part[...] + w_got[...]) * (2.0 * SCALE), (freq_v[0], freq_v[1]))
    lifted = jnp.concatenate([lifted[:, :WINDOW], lifted[:, WINDOW:]], axis=0)
    hi, lo = split(lifted)
    edge_place = pl.ds(pl.multiple_of(TILE + kern * HALO, HALO), HALO)
    own_rows = place(pl.ds(half_at, HALF), direct)
    grad = table_by_rows(block_of(own_rows, place(edge_place, direct), 0), hi, lo)
    g_v[...] = grad[HALF:, :TILE]
    first, second = fold(grad[:64, TILE:], grad[64:HALF, TILE:])
    g_side[0] = first
    g_side[1] = second
    first, second = fold(grad[HALF : HALF + 32, TILE:], grad[HALF + 32 :, TILE:])
    g_diag[0] = first
    g_diag[1] = second
    margin = exchange(g_v, g_side, g_diag, gg_v, gg_side, gg_diag, g_send, g_recv)
    each(margin, 0, lambda c: c.start())
    out_half[...] = grad[:HALF, :TILE]
    each(margin, 1, lambda c: c.wait_recv())

    def added(x, lanes):
        mine = lax.broadcasted_iota(jnp.int32, lanes.shape, 1) < HALO
        zero = jnp.zeros(lanes.shape, F32)
        return x + jnp.concatenate([jnp.where(mine, lanes, zero), jnp.where(mine, zero, lanes)], axis=1)

    top, bottom = fold(gg_side[0], gg_side[1])
    out_half[...] = added(out_half[...], jnp.concatenate([top, bottom], axis=0))
    top, bottom = fold(gg_diag[0], gg_diag[1])
    near = pl.ds(pl.multiple_of(kern * HALO, HALO), HALO)
    out_half[near, :] = out_half[near, :] + added(gg_v[...], jnp.concatenate([top, bottom], axis=0))

    mine = grad_h.at[pl.ds(half_at, HALF)]
    g_copy = remote(out_half, mine, p_send, p_recv, 4, partner)
    g_copy.start()
    store = pltpu.make_async_copy(out_half, mine, store_sem.at[2])
    store.start()
    stores.append(store)

    each(halo, 0, lambda c: c.wait_send())
    each(margin, 0, lambda c: c.wait_send())
    for copy in i_copies:
        copy.wait_send()
    w_copy.wait_send()
    for store in stores:
        store.wait()
    g_copy.wait()


def on_device(mask, target, spectra):
    tables = make_tables()
    kernels = spectra.shape[1]
    vmem = lambda shape, dtype=F32: pltpu.VMEM(shape, dtype)
    dma = lambda n: pltpu.SemaphoreType.DMA((n,))
    scratch = [
        vmem((TILE, TILE)), vmem((TILE, TILE), jnp.int32), vmem(spectra.shape),
        *[vmem(t.shape, BF16) for t in tables],
        vmem((2, 64, 128)), vmem((2, 32, 128)),
        vmem((HALO, TILE)), vmem((2, 64, 128)), vmem((2, 32, 128)),
        vmem((HALF, TILE)), vmem((2, TILE, TILE), BF16),
        vmem((BAND, 2 * BAND)), vmem((BAND, 2 * BAND)),
        vmem((kernels, 2 * TILE, TILE), BF16), vmem((2, kernels, TILE, TILE)),
        vmem((2, HALF, TILE)), vmem((2, HALF, TILE)), vmem((HALF, TILE)), vmem((TILE, TILE)),
        vmem((kernels, 2 * TILE, TILE), BF16), vmem((BAND, 2 * BAND)), vmem((BAND, 2 * BAND)),
        vmem((HALO, TILE)), vmem((2, 64, 128)), vmem((2, 32, 128)),
        vmem((HALO, TILE)), vmem((2, 64, 128)), vmem((2, 32, 128)),
        vmem((HALF, TILE)),
        dma(5), dma(3), dma(5), dma(5), dma(5), dma(5), dma(5), dma(5),
    ]
    anywhere = pl.BlockSpec(memory_space=pl.ANY)
    return pl.pallas_call(
        body,
        out_shape=[jax.ShapeDtypeStruct((TILE, TILE), F32)] * 2,
        in_specs=[anywhere] * (3 + len(tables)),
        out_specs=[anywhere] * 2,
        scratch_shapes=scratch,
        compiler_params=pltpu.CompilerParams(
            collective_id=0, has_side_effects=True, vmem_limit_bytes=60 * 1024 * 1024
        ),
        name="socs_step",
    )(mask, target, spectra, *[jnp.asarray(t) for t in tables])


def solution(mesh):
    return jax.shard_map(
        on_device,
        mesh=mesh,
        in_specs=(P("ty", "tx"), P("ty", "tx"), P(None, "kern", None, None)),
        out_specs=(P("ty", "tx"), P("ty", "tx")),
        check_vma=False,
    )
```

profile of v0, /device:TPU:39, one launch (start us, length us, event | category | flops | bytes accessed | tf_op | source)
XLA Modules:
  0.0 45.0 jit_solution(10966339684529283839)
XLA Ops:
  0.6 41.0 %socs_step.1 = (f32[256,256]{1,0:T(8,128)}, f32[256,256]{1,0:T(8,128)}) custom-call(f32[256,256]{1,0:T(8,128)} %mask_h.1, s32[256,256]{1,0:T(8,128)} %target_h.1, f32[2,12,128,128]{3,2,1,0:T(8,128)} %spec_h.1, bf16[2,384,512]{2,1,0:T(8,128)(2,1)} %constant.4.clone.place_h, bf16[2,256,768]{2,1,0:T(8,128)(2,1)} %constant.5.clone.freq_h), custom_call_target="tpu_custom_call" | custom-call | tf_op jit(solution)/shard_map/socs_step/pallas_call | solution.py:365
  41.6 1.7 %copy.9 = f32[256,256]{1,0:T(8,128)} copy(f32[256,256]{1,0:T(8,128)} %get-tuple-element.4) | data formatting | bytes 524288
  43.3 1.7 %copy.10 = f32[256,256]{1,0:T(8,128)} copy(f32[256,256]{1,0:T(8,128)} %get-tuple-element.5) | data formatting | bytes 524288
where the time goes:
time: 45.1 us; the launch traced here: 45 us
  Pallas kernels  41 us (91%)
  local copies, waits for them, and re-layouts  3.34 us (7%)
  between operations  0.64 us (1%)
    pallas_call x1, Pallas kernels, on_device(): pl.pallas_call(body, out_shape=[jax.ShapeDtypeStruct((TILE, TILE), F32)]...  41 us
    unnamed x2, local copies, waits for them, and re-layouts  3.34 us

commit v1 on v0

--- a/solution.py
+++ b/solution.py
@@ -15,7 +15,6 @@
 HALF = TILE // 2
 STEEP = 8.0
 LEVEL = 1.0
-UNROLL = 2
 SCALE = 1.0 / (WINDOW * WINDOW)
 MESH = pl.DeviceIdType.MESH
 F32 = jnp.float32
@@ -179,7 +178,7 @@
                 act(copy)
 
     halo = exchange(
-        mask_v.at[pl.ds(edge_at, HALO)], send_side, send_diag, got_v, got_side, got_diag,
+        mask_h.at[pl.ds(edge_at, HALO)], send_side, send_diag, got_v, got_side, got_diag,
         h_send, h_recv,
     )
     each(halo, 0, lambda c: c.start())
@@ -220,12 +219,8 @@
     kernels = spec_v.shape[1]
 
     def loop(step):
-        def several(i, carry):
-            for j in range(UNROLL):
-                step(i * UNROLL + j)
-            return carry
-
-        lax.fori_loop(0, kernels // UNROLL, several, 0)
+        for k in range(kernels):
+            step(k)
 
     def to_columns(k):
         f_re, f_im = w_part[:, :BAND], w_part[:, BAND:]
@@ -300,17 +295,18 @@
     hi, lo = split(lifted)
     edge_place = pl.ds(pl.multiple_of(TILE + kern * HALO, HALO), HALO)
     own_rows = place(pl.ds(half_at, HALF), direct)
-    grad = table_by_rows(block_of(own_rows, place(edge_place, direct), 0), hi, lo)
-    g_v[...] = grad[HALF:, :TILE]
-    first, second = fold(grad[:64, TILE:], grad[64:HALF, TILE:])
+    edge_grad = table_by_rows(place(edge_place, direct), hi, lo)
+    side_grad = table_by_rows(own_rows, hi[:, TILE:], lo[:, TILE:])
+    g_v[...] = edge_grad[:, :TILE]
+    first, second = fold(side_grad[:64], side_grad[64:])
     g_side[0] = first
     g_side[1] = second
-    first, second = fold(grad[HALF : HALF + 32, TILE:], grad[HALF + 32 :, TILE:])
+    first, second = fold(edge_grad[:32, TILE:], edge_grad[32:, TILE:])
     g_diag[0] = first
     g_diag[1] = second
     margin = exchange(g_v, g_side, g_diag, gg_v, gg_side, gg_diag, g_send, g_recv)
     each(margin, 0, lambda c: c.start())
-    out_half[...] = grad[:HALF, :TILE]
+    out_half[...] = table_by_rows(own_rows, hi[:, :TILE], lo[:, :TILE])
     each(margin, 1, lambda c: c.wait_recv())
 
     def added(x, lanes):
@@ -362,17 +358,23 @@
         dma(5), dma(3), dma(5), dma(5), dma(5), dma(5), dma(5), dma(5),
     ]
     anywhere = pl.BlockSpec(memory_space=pl.ANY)
-    return pl.pallas_call(
+    outs = pl.pallas_call(
         body,
         out_shape=[jax.ShapeDtypeStruct((TILE, TILE), F32)] * 2,
         in_specs=[anywhere] * (3 + len(tables)),
         out_specs=[anywhere] * 2,
         scratch_shapes=scratch,
         compiler_params=pltpu.CompilerParams(
-            collective_id=0, has_side_effects=True, vmem_limit_bytes=60 * 1024 * 1024
+            collective_id=0, has_side_effects=True, vmem_limit_bytes=25165824
         ),
         name="socs_step",
-    )(mask, target, spectra, *[jnp.asarray(t) for t in tables])
+    )(*[pltpu.with_memory_space_constraint(x, pltpu.HBM) for x in (mask, target, spectra, *map(jnp.asarray, tables))])
+
+    def put(a, b, c, d):
+        c[...] = a[...]
+        d[...] = b[...]
+
+    return pl.pallas_call(put, out_shape=[jax.ShapeDtypeStruct((TILE, TILE), F32)] * 2, name="put", compiler_params=pltpu.CompilerParams(vmem_limit_bytes=4 * 1024 * 1024))(*outs)
 
 
 def solution(mesh):

time: 45.1 us -> 37.9 us (0.84)
  Pallas kernels: 41 us -> 37.2 us
  local copies, waits for them, and re-layouts: 3.34 us -> 0 us
    pallas_call x1, Pallas kernels: 41 us -> 36.4 us  [on_device(): pl.pallas_call(body, out_shape=[jax.ShapeDtypeStruct((TILE, TILE), F32)]...]
    unnamed x2 -> x0, local copies, waits for them, and re-layouts: 3.34 us -> none
    pallas_call x0 -> x1, Pallas kernels: none -> 0.82 us  [on_device(): pl.pallas_call(put, out_shape=[jax.ShapeDtypeStruct((TILE, TILE), F32)] *...]
where the time goes in v1:
time: 37.9 us; the launch traced here: 37.8 us
  Pallas kernels  37.2 us (98%)
  between operations  0.64 us (2%)
    pallas_call x1, Pallas kernels, on_device(): pl.pallas_call(body, out_shape=[jax.ShapeDtypeStruct((TILE, TILE), F32)]...  36.4 us
    pallas_call x1, Pallas kernels, on_device(): pl.pallas_call(put, out_shape=[jax.ShapeDtypeStruct((TILE, TILE), F32)] *...  0.82 us

profile of v1, /device:TPU:39, one launch (start us, length us, event | category | flops | bytes accessed | tf_op | source)
XLA Modules:
  0.0 37.8 jit_solution(1521346007322947443)
XLA Ops:
  0.6 36.4 %socs_step.1 = (f32[256,256]{1,0:T(8,128)S(1)}, f32[256,256]{1,0:T(8,128)S(1)}) custom-call(f32[256,256]{1,0:T(8,128)} %mask_h.1, s32[256,256]{1,0:T(8,128)} %target_h.1, f32[2,12,128,128]{3,2,1,0:T(8,128)} %spec_h.1, bf16[2,384,512]{2,1,0:T(8,128)(2,1)} %constant.4.clone.place_h, bf16[2,256,768]{2,1,0:T(8,128)(2,1)} %constant.5.clone.freq_h), custom_call_target="tpu_custom_call" | custom-call | tf_op jit(solution)/shard_map/socs_step/pallas_call | solution.py:361
  37.0 0.8 %put.1 = (f32[256,256]{1,0:T(8,128)}, f32[256,256]{1,0:T(8,128)}) custom-call(f32[256,256]{1,0:T(8,128)S(1)} %get-tuple-element.4.a, f32[256,256]{1,0:T(8,128)S(1)} %get-tuple-element.5.b), custom_call_target="tpu_custom_call" | custom-call | tf_op jit(solution)/shard_map/put/pallas_call | solution.py:377

commit v2 on v1

v2 whole, which is shorter than its diff:
```python
import math

import jax
import jax.numpy as jnp
import numpy as np
from jax import lax
from jax.experimental import pallas as pl
from jax.experimental.pallas import tpu as pltpu
from jax.sharding import PartitionSpec as P

TILE = 256
HALO = 64
BAND = 128
WINDOW = TILE + 2 * HALO
HALF = TILE // 2
STEEP = 8.0
LEVEL = 1.0
SCALE = 1.0 / (WINDOW * WINDOW)
MESH = pl.DeviceIdType.MESH
F32 = jnp.float32
BF16 = jnp.bfloat16


def halves(table):
    table = np.asarray(table, np.float32)
    hi = table.astype(BF16)
    lo = (table - hi.astype(np.float32)).astype(BF16)
    return hi, lo


def make_tables():
    freq = np.arange(BAND) - BAND // 2
    order = np.concatenate(
        [np.arange(TILE) + HALO, np.arange(HALO), np.arange(HALO) + HALO + TILE]
    )

    def waves(places):
        angle = np.mod(places[:, None] * freq[None, :], 2 * WINDOW) * (math.pi / WINDOW)
        return np.cos(angle), np.sin(angle)

    c, s = waves(2 * order - (WINDOW - 1))
    by_place = np.concatenate([c, -s], 1)
    by_freq = np.block([[c.T, s.T], [-s.T, c.T]])
    c, s = waves(2 * np.arange(HALF) + 1)
    fold_place = np.concatenate([c, s], 1)
    fold_freq = np.concatenate([c.T, s.T], 1)
    return [np.stack(halves(t)) for t in (by_place, by_freq, fold_place, fold_freq)]


def split(x):
    hi = x.astype(BF16)
    return hi, (x - hi.astype(F32)).astype(BF16)


def dot(a, b):
    return jnp.dot(a, b, preferred_element_type=F32)


def rows_by_table(x, table):
    hi, lo = split(x)
    t_hi, t_lo = table
    left = jnp.concatenate([hi, lo, hi], axis=1)
    return dot(left, jnp.concatenate([t_hi, t_hi, t_lo], axis=0))


def table_by_rows(table, hi, lo):
    t_hi, t_lo = table
    left = jnp.concatenate([t_hi, t_hi, t_lo], axis=1)
    return dot(left, jnp.concatenate([hi, lo, hi], axis=0))


def place_of(order, blocks):
    size = TILE // (2 * blocks)
    block, inside = order // (2 * size), order % (2 * size)
    return jnp.where(inside < size, HALF + block * size + inside, HALF - 1 - block * size - (inside - size))


def reorder(blocks, to_folded):
    rows = lax.broadcasted_iota(jnp.int32, (TILE, TILE), 0)
    lanes = lax.broadcasted_iota(jnp.int32, (TILE, TILE), 1)
    hit = (place_of(rows, blocks) == lanes) if to_folded else (rows == place_of(lanes, blocks))
    return hit.astype(F32).astype(BF16)


def fold(a, b):
    left_lanes = lax.broadcasted_iota(jnp.int32, a.shape, 1) < HALO
    first = jnp.where(left_lanes, a, pltpu.roll(b, HALO, 1))
    second = jnp.where(left_lanes, pltpu.roll(a, HALO, 1), b)
    return first, second


def body(
    mask_h, target_h, spec_h, place_h, freq_h, fplace_h, ffreq_h,
    resist_h, grad_h,
    mask_v, target_v, spec_v, place_v, freq_v, fplace_v, ffreq_v,
    send_side, send_diag, got_v, got_side, got_diag,
    acc_half, a_stack, f_part, f_got, r_stack, field, inten, inten_got, weight, goal, resist_p, resist_v,
    c_stack, w_part, w_got, g_v, g_side, g_diag, gg_v, gg_side, gg_diag, out_half,
    load_sem, store_sem, h_send, h_recv, p_send, p_recv, g_send, g_recv,
):
    kern, ty, tx = lax.axis_index("kern"), lax.axis_index("ty"), lax.axis_index("tx")
    n_ty, n_tx = lax.axis_size("ty"), lax.axis_size("tx")
    other = 1 - kern
    vt = ty - 1 + 2 * kern
    has_v = jnp.logical_and(vt >= 0, vt < n_ty)
    has_l, has_r = tx > 0, tx < n_tx - 1
    has_dl, has_dr = jnp.logical_and(has_v, has_l), jnp.logical_and(has_v, has_r)
    partner = (other, ty, tx)
    vertical = (other, vt, tx)
    left, right = (kern, ty, tx - 1), (kern, ty, tx + 1)
    diag_l, diag_r = (other, vt, tx - 1), (other, vt, tx + 1)
    peers = [(has_v, vertical), (has_l, left), (has_r, right), (has_dl, diag_l), (has_dr, diag_r)]

    barrier = pltpu.get_barrier_semaphore()
    pl.semaphore_signal(barrier, inc=1, device_id=partner, device_id_type=MESH)
    for has, peer in peers:

        @pl.when(has)
        def _(peer=peer):
            pl.semaphore_signal(barrier, inc=1, device_id=peer, device_id_type=MESH)

    loads = [
        (mask_h, mask_v), (place_h, place_v), (freq_h, freq_v), (spec_h, spec_v), (ffreq_h, ffreq_v),
        (fplace_h, fplace_v), (target_h, target_v),
    ]
    loads = [pltpu.make_async_copy(a, b, load_sem.at[i]) for i, (a, b) in enumerate(loads)]
    for load in loads:
        load.start()
    l_mask, l_place, l_freq, l_spec, l_ffreq, l_fplace, l_target = loads

    def place(rows, lanes):
        return place_v[0, rows, lanes], place_v[1, rows, lanes]

    def block_of(first, second, axis):
        return tuple(jnp.concatenate([a, b], axis=axis) for a, b in zip(first, second))

    inner, direct = slice(0, TILE), slice(0, 2 * BAND)
    edges = slice(TILE, WINDOW)

    a_stack[...] = jnp.zeros(a_stack.shape, BF16)
    for has, bufs in (
        (has_v, (got_v, gg_v)),
        (has_l, (got_side.at[0], gg_side.at[0])),
        (has_r, (got_side.at[1], gg_side.at[1])),
        (has_dl, (got_diag.at[0], gg_diag.at[0])),
        (has_dr, (got_diag.at[1], gg_diag.at[1])),
    ):

        @pl.when(jnp.logical_not(has))
        def _(bufs=bufs):
            for buf in bufs:
                buf[...] = jnp.zeros(buf.shape, F32)

    half_at = pl.multiple_of(kern * HALF, HALF)
    edge_at = pl.multiple_of(kern * (TILE - HALO), HALO)
    l_mask.wait()
    mask_half = mask_v[pl.ds(half_at, HALF), :]
    mask_edge = mask_v[pl.ds(edge_at, HALO), :]

    def side_lanes(x):
        lanes = lax.broadcasted_iota(jnp.int32, (x.shape[0], 128), 1) < HALO
        return jnp.where(lanes, x[:, :128], x[:, 128:])

    corners = side_lanes(mask_edge)
    first, second = fold(corners[:32], corners[32:])
    send_diag[0] = first
    send_diag[1] = second
    sides = side_lanes(mask_half)
    first, second = fold(sides[:64], sides[64:])
    send_side[0] = first
    send_side[1] = second

    pl.semaphore_wait(barrier, 1 + sum(has.astype(jnp.int32) for has, _ in peers))

    def remote(src, dst, send, recv, at, peer):
        return pltpu.make_async_remote_copy(
            src_ref=src, dst_ref=dst, send_sem=send.at[at], recv_sem=recv.at[at],
            device_id=peer, device_id_type=MESH,
        )

    def exchange(src_v, src_side, src_diag, dst_v, dst_side, dst_diag, send, recv):
        return (
            [
                (has_dl, has_dr, remote(src_diag.at[0], dst_diag.at[1], send, recv, 3, diag_l)),
                (has_dr, has_dl, remote(src_diag.at[1], dst_diag.at[0], send, recv, 4, diag_r)),
            ],
            [(has_v, has_v, remote(src_v, dst_v, send, recv, 0, vertical))],
            [
                (has_l, has_r, remote(src_side.at[0], dst_side.at[1], send, recv, 1, left)),
                (has_r, has_l, remote(src_side.at[1], dst_side.at[0], send, recv, 2, right)),
            ],
        )

    def each(copies, which, act):
        for entry in copies:

            @pl.when(entry[which])
            def _(copy=entry[2]):
                act(copy)

    h_diag, h_vert, h_side = exchange(
        mask_h.at[pl.ds(edge_at, HALO)], send_side, send_diag, got_v, got_side, got_diag,
        h_send, h_recv,
    )
    start = lambda c: c.start()
    arrived = lambda c: c.wait_recv()
    each(h_diag + h_vert + h_side, 0, start)

    l_place.wait()
    own = place(inner, direct)
    acc_half[...] = rows_by_table(mask_half, own)
    l_freq.wait()
    each(h_side, 1, arrived)
    top, bottom = fold(got_side[0], got_side[1])
    side_part = rows_by_table(jnp.concatenate([top, bottom], axis=0), place(edges, direct))
    half_hi, half_lo = split(acc_half[...] + side_part)
    a_stack[0, pl.ds(0, HALF), :] = half_hi
    a_stack[1, pl.ds(0, HALF), :] = half_lo
    each(h_vert, 1, arrived)
    g_v[...] = rows_by_table(got_v[...], own)
    each(h_diag, 1, arrived)
    top, bottom = fold(got_diag[0], got_diag[1])
    strip = g_v[...] + rows_by_table(jnp.concatenate([top, bottom], axis=0), place(edges, direct))
    edge_rows = pl.ds(pl.multiple_of(HALF + kern * HALO, HALO), HALO)
    for part, edge in enumerate(split(strip)):
        a_stack[part, edge_rows, :] = edge
    half_lanes = pl.ds(half_at, HALF)
    own_y = []
    for part in range(2):
        cos = [freq_v[part, pl.ds(0, BAND), half_lanes], freq_v[part, :BAND, TILE:WINDOW]]
        sin_lanes = pl.ds(pl.multiple_of(WINDOW + half_at, HALF), HALF)
        sin = [freq_v[part, pl.ds(0, BAND), sin_lanes], freq_v[part, :BAND, WINDOW + TILE :]]
        own_y.append(jnp.concatenate([jnp.concatenate(cos, axis=1), jnp.concatenate(sin, axis=1)], axis=0))
    full = table_by_rows(own_y, a_stack[0], a_stack[1])
    f_part[:, :BAND] = full[:BAND, :BAND] + full[BAND:, BAND:]
    f_part[:, BAND:] = full[:BAND, BAND:] - full[BAND:, :BAND]
    f_copy = remote(f_part, f_got, p_send, p_recv, 0, partner)
    f_copy.start()
    l_target.wait()
    folded = dot(reorder(2, True), target_v[...].astype(F32).astype(BF16))
    goal[...] = dot(folded.astype(BF16), reorder(1, False))
    l_spec.wait()
    l_ffreq.wait()
    l_fplace.wait()
    f_copy.wait_recv()
    w_part[...] = (f_part[...] + f_got[...]) * SCALE

    kernels = spec_v.shape[1]

    def loop(step):
        for k in range(kernels):
            step(k)

    def to_columns(k):
        f_re, f_im = w_part[:, :BAND], w_part[:, BAND:]
        h_re, h_im = spec_v[0, k], spec_v[1, k]
        prod = jnp.concatenate([f_re * h_re - f_im * h_im, f_re * h_im + f_im * h_re], axis=0)
        value = rows_by_table(prod, (ffreq_v[0], ffreq_v[1]))
        re_c, re_s, im_c, im_s = value[:BAND, :HALF], value[:BAND, HALF:], value[BAND:, :HALF], value[BAND:, HALF:]
        hi, lo = split(jnp.concatenate([re_c - im_s, re_c + im_s, im_c + re_s, im_c - re_s], axis=1))
        r_stack[k, pl.ds(0, BAND), :] = hi
        r_stack[k, pl.ds(BAND, BAND), :] = lo

    loop(to_columns)

    i_copies = []
    for b in range(2):
        inten[b] = jnp.zeros((HALF, TILE), F32)

        def to_rows(k, b=b):
            at = slice(b * 64, b * 64 + 64)
            hi, lo = r_stack[k, pl.ds(0, BAND), :], r_stack[k, pl.ds(BAND, BAND), :]
            table = [jnp.concatenate([fplace_v[p, at, :BAND], fplace_v[p, at, BAND:]], axis=0) for p in range(2)]
            value = table_by_rows(table, hi, lo)
            c_re, c_im, s_re, s_im = value[:64, :TILE], value[:64, TILE:], value[64:, :TILE], value[64:, TILE:]
            re = jnp.concatenate([c_re - s_im, c_re + s_im], axis=0)
            im = jnp.concatenate([c_im + s_re, c_im - s_re], axis=0)
            field[b, k, pl.ds(0, HALF), :] = re
            field[b, k, pl.ds(HALF, HALF), :] = im
            inten[b] += re * re + im * im

        loop(to_rows)
        copy = remote(inten.at[b], inten_got.at[b], p_send, p_recv, 1 + b, partner)
        copy.start()
        i_copies.append(copy)

    stores = []
    for b in range(2):
        i_copies[b].wait_recv()
        rows = pl.ds(b * HALF, HALF)
        resist = jax.nn.sigmoid(STEEP * (inten[b] + inten_got[b] - LEVEL))
        resist_p[rows, :] = resist
        weight[...] = 2.0 * (resist - goal[rows, :]) * STEEP * resist * (1.0 - resist)

        def back_columns(k, b=b):
            w = weight[...]
            re, im = w * field[b, k, pl.ds(0, HALF), :], w * field[b, k, pl.ds(HALF, HALF), :]
            even_re, odd_re = re[:, :HALF] + re[:, HALF:], re[:, HALF:] - re[:, :HALF]
            even_im, odd_im = im[:, :HALF] + im[:, HALF:], im[:, :HALF] - im[:, HALF:]
            hi, lo = split(
                jnp.concatenate(
                    [jnp.concatenate([even_re, odd_im], axis=1), jnp.concatenate([even_im, odd_re], axis=1)], axis=0
                )
            )
            cos = jnp.concatenate([fplace_v[0, :, :BAND], fplace_v[1, :, :BAND]], axis=1)
            sin = jnp.concatenate([fplace_v[0, :, BAND:], fplace_v[1, :, BAND:]], axis=1)
            value = dot(jnp.concatenate([hi, lo], axis=1), jnp.concatenate([cos, sin, cos, sin], axis=0))
            value = value[:, :BAND] + value[:, BAND:]
            p_re, m_re, p_im, m_im = value[:64], value[64:HALF], value[HALF : HALF + 64], value[HALF + 64 :]
            even = jnp.concatenate([p_re + m_re, p_im + m_im], axis=1)
            odd = jnp.concatenate([p_im - m_im, m_re - p_re], axis=1)
            for at, part in ((0, even), (HALF, odd)):
                hi, lo = split(part)
                c_stack[k, pl.ds(at + b * 64, 64), :] = hi
                c_stack[k, pl.ds(TILE + at + b * 64, 64), :] = lo

        loop(back_columns)

    f_copy.wait_send()
    f_part[...] = jnp.zeros((BAND, 2 * BAND), F32)

    def back_rows(k):
        hi, lo = c_stack[k, pl.ds(0, TILE), :], c_stack[k, pl.ds(TILE, TILE), :]
        value = table_by_rows((ffreq_v[0], ffreq_v[1]), hi, lo)
        s_re, s_im = value[:, :BAND], value[:, BAND:]
        h_re, h_im = spec_v[0, k], spec_v[1, k]
        f_part[:, :BAND] += h_re * s_re + h_im * s_im
        f_part[:, BAND:] += h_re * s_im - h_im * s_re

    loop(back_rows)
    w_copy = remote(f_part, w_got, p_send, p_recv, 3, partner)
    w_copy.start()
    high = resist_p[...].astype(BF16)
    rest = resist_p[...] - high.astype(F32)
    mid, low = split(rest)
    moved = dot(reorder(2, False), jnp.concatenate([high, mid, low], axis=1)).astype(BF16)
    lanes = reorder(1, True)
    resist_v[...] = dot(moved, jnp.concatenate([lanes, lanes, lanes], axis=0))
    store = pltpu.make_async_copy(resist_v, resist_h, store_sem.at[0])
    store.start()
    stores.append(store)
    w_copy.wait_recv()

    lifted = rows_by_table((f_part[...] + w_got[...]) * (2.0 * SCALE), (freq_v[0], freq_v[1]))
    lifted = jnp.concatenate([lifted[:, :WINDOW], lifted[:, WINDOW:]], axis=0)
    hi, lo = split(lifted)
    edge_place = pl.ds(pl.multiple_of(TILE + kern * HALO, HALO), HALO)
    own_rows = place(pl.ds(half_at, HALF), direct)
    edge_grad = table_by_rows(place(edge_place, direct), hi, lo)
    g_diag[...] = jnp.stack(fold(edge_grad[:32, TILE:], edge_grad[32:, TILE:]))
    g_v[...] = edge_grad[:, :TILE]
    m_diag, m_vert, m_side = exchange(g_v, g_side, g_diag, gg_v, gg_side, gg_diag, g_send, g_recv)
    each(m_diag + m_vert, 0, start)
    side_grad = table_by_rows(own_rows, hi[:, TILE:], lo[:, TILE:])
    g_side[...] = jnp.stack(fold(side_grad[:64], side_grad[64:]))
    each(m_side, 0, start)
    out_half[...] = table_by_rows(own_rows, hi[:, :TILE], lo[:, :TILE])
    each(m_side, 1, arrived)

    def added(x, lanes):
        mine = lax.broadcasted_iota(jnp.int32, lanes.shape, 1) < HALO
        zero = jnp.zeros(lanes.shape, F32)
        return x + jnp.concatenate([jnp.where(mine, lanes, zero), jnp.where(mine, zero, lanes)], axis=1)

    top, bottom = fold(gg_side[0], gg_side[1])
    out_half[...] = added(out_half[...], jnp.concatenate([top, bottom], axis=0))
    near = pl.ds(pl.multiple_of(kern * HALO, HALO), HALO)
    far = pl.ds(pl.multiple_of(other * HALO, HALO), HALO)
    near_h = pl.ds(pl.multiple_of(half_at + kern * HALO, HALO), HALO)
    far_h = pl.ds(pl.multiple_of(half_at + other * HALO, HALO), HALO)
    g_copies = []

    def give(at, at_h, n):
        g_copies.append(remote(out_half.at[at], grad_h.at[at_h], p_send, p_recv, n, partner))
        g_copies[-1].start()
        stores.append(pltpu.make_async_copy(out_half.at[at], grad_h.at[at_h], store_sem.at[n - 3]))
        stores[-1].start()

    give(far, far_h, 4)
    each(m_vert, 1, arrived)
    out_half[near, :] = out_half[near, :] + gg_v[...]
    each(m_diag, 1, arrived)
    top, bottom = fold(gg_diag[0], gg_diag[1])
    out_half[near, :] = added(out_half[near, :], jnp.concatenate([top, bottom], axis=0))
    give(near, near_h, 5)

    each(h_diag + h_vert + h_side + m_diag + m_vert + m_side, 0, lambda c: c.wait_send())
    for copy in i_copies:
        copy.wait_send()
    w_copy.wait_send()
    for store in stores:
        store.wait()
    for copy in g_copies:
        copy.wait()


def on_device(mask, target, spectra):
    tables = make_tables()
    kernels = spectra.shape[1]
    vmem = lambda shape, dtype=F32: pltpu.VMEM(shape, dtype)
    dma = lambda n: pltpu.SemaphoreType.DMA((n,))
    scratch = [
        vmem((TILE, TILE)), vmem((TILE, TILE), jnp.int32), vmem(spectra.shape),
        *[vmem(t.shape, BF16) for t in tables],
        vmem((2, 64, 128)), vmem((2, 32, 128)),
        vmem((HALO, TILE)), vmem((2, 64, 128)), vmem((2, 32, 128)),
        vmem((HALF, TILE)), vmem((2, TILE, TILE), BF16),
        vmem((BAND, 2 * BAND)), vmem((BAND, 2 * BAND)),
        vmem((kernels, 2 * BAND, 2 * TILE), BF16), vmem((2, kernels, TILE, TILE)),
        vmem((2, HALF, TILE)), vmem((2, HALF, TILE)), vmem((HALF, TILE)), vmem((TILE, TILE)), vmem((TILE, TILE)), vmem((TILE, TILE)),
        vmem((kernels, 2 * TILE, TILE), BF16), vmem((BAND, 2 * BAND)), vmem((BAND, 2 * BAND)),
        vmem((HALO, TILE)), vmem((2, 64, 128)), vmem((2, 32, 128)),
        vmem((HALO, TILE)), vmem((2, 64, 128)), vmem((2, 32, 128)),
        vmem((HALF, TILE)),
        dma(7), dma(3), dma(5), dma(5), dma(6), dma(6), dma(5), dma(5),
    ]
    anywhere = pl.BlockSpec(memory_space=pl.ANY)
    outs = pl.pallas_call(
        body,
        out_shape=[jax.ShapeDtypeStruct((TILE, TILE), F32)] * 2,
        in_specs=[anywhere] * (3 + len(tables)),
        out_specs=[anywhere] * 2,
        scratch_shapes=scratch,
        compiler_params=pltpu.CompilerParams(
            collective_id=0, has_side_effects=True, vmem_limit_bytes=25165824
        ),
        name="socs_step",
    )(*[pltpu.with_memory_space_constraint(x, pltpu.HBM) for x in (mask, target, spectra, *map(jnp.asarray, tables))])

    def put(a, b, c, d):
        c[...] = a[...]
        d[...] = b[...]

    return pl.pallas_call(put, out_shape=[jax.ShapeDtypeStruct((TILE, TILE), F32)] * 2, name="put", compiler_params=pltpu.CompilerParams(vmem_limit_bytes=4 * 1024 * 1024))(*outs)


def solution(mesh):
    return jax.shard_map(
        on_device,
        mesh=mesh,
        in_specs=(P("ty", "tx"), P("ty", "tx"), P(None, "kern", None, None)),
        out_specs=(P("ty", "tx"), P("ty", "tx")),
        check_vma=False,
    )
```

time: 37.9 us -> 32.5 us (0.86)
  Pallas kernels: 37.2 us -> 31.8 us
    pallas_call x1, Pallas kernels: 36.4 us -> 30.9 us  [on_device(): pl.pallas_call(body, out_shape=[jax.ShapeDtypeStruct((TILE, TILE), F32)]...]
where the time goes in v2:
time: 32.5 us; the launch traced here: 32.4 us
  Pallas kernels  31.8 us (98%)
  between operations  0.64 us (2%)
    pallas_call x1, Pallas kernels, on_device(): pl.pallas_call(body, out_shape=[jax.ShapeDtypeStruct((TILE, TILE), F32)]...  30.9 us
    pallas_call x1, Pallas kernels, on_device(): pl.pallas_call(put, out_shape=[jax.ShapeDtypeStruct((TILE, TILE), F32)] *...  0.82 us

profile of v2, /device:TPU:39, one launch (start us, length us, event | category | flops | bytes accessed | tf_op | source)
XLA Modules:
  0.0 32.4 jit_solution(2213928165855176945)
XLA Ops:
  0.6 30.9 %socs_step.1 = (f32[256,256]{1,0:T(8,128)S(1)}, f32[256,256]{1,0:T(8,128)S(1)}) custom-call(f32[256,256]{1,0:T(8,128)} %mask_h.1, s32[256,256]{1,0:T(8,128)} %target_h.1, f32[2,12,128,128]{3,2,1,0:T(8,128)} %spec_h.1, bf16[2,384,256]{2,1,0:T(8,128)(2,1)} %constant.8.clone.place_h, bf16[2,256,768]{2,1,0:T(8,128)(2,1)} %constant.9.clone.freq_h, ...), custom_call_target="tpu_custom_call" | custom-call | tf_op jit(solution)/shard_map/socs_step/pallas_call | solution.py:418
  31.6 0.8 %put.1 = (f32[256,256]{1,0:T(8,128)}, f32[256,256]{1,0:T(8,128)}) custom-call(f32[256,256]{1,0:T(8,128)S(1)} %get-tuple-element.4.a, f32[256,256]{1,0:T(8,128)S(1)} %get-tuple-element.5.b), custom_call_target="tpu_custom_call" | custom-call | tf_op jit(solution)/shard_map/put/pallas_call | solution.py:434

commit v3 on v2

--- a/solution.py
+++ b/solution.py
@@ -111,45 +111,29 @@
     diag_l, diag_r = (other, vt, tx - 1), (other, vt, tx + 1)
     peers = [(has_v, vertical), (has_l, left), (has_r, right), (has_dl, diag_l), (has_dr, diag_r)]
 
-    barrier = pltpu.get_barrier_semaphore()
-    pl.semaphore_signal(barrier, inc=1, device_id=partner, device_id_type=MESH)
-    for has, peer in peers:
-
-        @pl.when(has)
-        def _(peer=peer):
-            pl.semaphore_signal(barrier, inc=1, device_id=peer, device_id_type=MESH)
-
     loads = [
         (mask_h, mask_v), (place_h, place_v), (freq_h, freq_v), (spec_h, spec_v), (ffreq_h, ffreq_v),
         (fplace_h, fplace_v), (target_h, target_v),
     ]
     loads = [pltpu.make_async_copy(a, b, load_sem.at[i]) for i, (a, b) in enumerate(loads)]
-    for load in loads:
+    loads[0].start()
+    barrier = pltpu.get_barrier_semaphore()
+    pl.semaphore_signal(barrier, inc=1, device_id=partner, device_id_type=MESH)
+    for has, peer in peers:
+
+        @pl.when(has)
+        def _(peer=peer):
+            pl.semaphore_signal(barrier, inc=1, device_id=peer, device_id_type=MESH)
+
+    for load in loads[1:]:
         load.start()
     l_mask, l_place, l_freq, l_spec, l_ffreq, l_fplace, l_target = loads
 
     def place(rows, lanes):
         return place_v[0, rows, lanes], place_v[1, rows, lanes]
 
-    def block_of(first, second, axis):
-        return tuple(jnp.concatenate([a, b], axis=axis) for a, b in zip(first, second))
-
     inner, direct = slice(0, TILE), slice(0, 2 * BAND)
     edges = slice(TILE, WINDOW)
-
-    a_stack[...] = jnp.zeros(a_stack.shape, BF16)
-    for has, bufs in (
-        (has_v, (got_v, gg_v)),
-        (has_l, (got_side.at[0], gg_side.at[0])),
-        (has_r, (got_side.at[1], gg_side.at[1])),
-        (has_dl, (got_diag.at[0], gg_diag.at[0])),
-        (has_dr, (got_diag.at[1], gg_diag.at[1])),
-    ):
-
-        @pl.when(jnp.logical_not(has))
-        def _(bufs=bufs):
-            for buf in bufs:
-                buf[...] = jnp.zeros(buf.shape, F32)
 
     half_at = pl.multiple_of(kern * HALF, HALF)
     edge_at = pl.multiple_of(kern * (TILE - HALO), HALO)
@@ -205,6 +189,21 @@
     start = lambda c: c.start()
     arrived = lambda c: c.wait_recv()
     each(h_diag + h_vert + h_side, 0, start)
+
+    a_stack[...] = jnp.zeros(a_stack.shape, BF16)
+    for has, bufs in (
+        (has_v, (got_v, gg_v)),
+        (has_l, (got_side.at[0], gg_side.at[0])),
+        (has_r, (got_side.at[1], gg_side.at[1])),
+        (has_dl, (got_diag.at[0], gg_diag.at[0])),
+        (has_dr, (got_diag.at[1], gg_diag.at[1])),
+    ):
+
+        @pl.when(jnp.logical_not(has))
+        def _(bufs=bufs):
+            for buf in bufs:
+                buf[...] = jnp.zeros(buf.shape, F32)
+
 
     l_place.wait()
     own = place(inner, direct)
@@ -341,20 +340,28 @@
     stores.append(store)
     w_copy.wait_recv()
 
-    lifted = rows_by_table((f_part[...] + w_got[...]) * (2.0 * SCALE), (freq_v[0], freq_v[1]))
-    lifted = jnp.concatenate([lifted[:, :WINDOW], lifted[:, WINDOW:]], axis=0)
-    hi, lo = split(lifted)
-    edge_place = pl.ds(pl.multiple_of(TILE + kern * HALO, HALO), HALO)
-    own_rows = place(pl.ds(half_at, HALF), direct)
-    edge_grad = table_by_rows(place(edge_place, direct), hi, lo)
+    both = split((f_part[...] + w_got[...]) * (2.0 * SCALE))
+
+    def lifted(rows):
+        table = [jnp.concatenate([place_v[p, rows, :BAND], place_v[p, rows, BAND:]], axis=0) for p in range(2)]
+        value = table_by_rows(table, *both)
+        n = value.shape[0] // 2
+        re = value[:n, :BAND] + value[n:, BAND:]
+        return jnp.concatenate([re, value[:n, BAND:] - value[n:, :BAND]], axis=1)
+
+    def spread(x, lanes):
+        return rows_by_table(x, (freq_v[0, :, lanes], freq_v[1, :, lanes]))
+
+    edge_grad = spread(lifted(pl.ds(pl.multiple_of(TILE + kern * HALO, HALO), HALO)), slice(0, WINDOW))
     g_diag[...] = jnp.stack(fold(edge_grad[:32, TILE:], edge_grad[32:, TILE:]))
     g_v[...] = edge_grad[:, :TILE]
     m_diag, m_vert, m_side = exchange(g_v, g_side, g_diag, gg_v, gg_side, gg_diag, g_send, g_recv)
     each(m_diag + m_vert, 0, start)
-    side_grad = table_by_rows(own_rows, hi[:, TILE:], lo[:, TILE:])
+    half_lift = lifted(pl.ds(half_at, HALF))
+    side_grad = spread(half_lift, slice(TILE, WINDOW))
     g_side[...] = jnp.stack(fold(side_grad[:64], side_grad[64:]))
     each(m_side, 0, start)
-    out_half[...] = table_by_rows(own_rows, hi[:, :TILE], lo[:, :TILE])
+    out_half[...] = spread(half_lift, slice(0, TILE))
     each(m_side, 1, arrived)
 
     def added(x, lanes):
@@ -427,11 +434,14 @@
         name="socs_step",
     )(*[pltpu.with_memory_space_constraint(x, pltpu.HBM) for x in (mask, target, spectra, *map(jnp.asarray, tables))])
 
-    def put(a, b, c, d):
-        c[...] = a[...]
-        d[...] = b[...]
-
-    return pl.pallas_call(put, out_shape=[jax.ShapeDtypeStruct((TILE, TILE), F32)] * 2, name="put", compiler_params=pltpu.CompilerParams(vmem_limit_bytes=4 * 1024 * 1024))(*outs)
+    def put(a, b, c, d, sem):
+        copies = [pltpu.make_async_copy(a, c, sem.at[0]), pltpu.make_async_copy(b, d, sem.at[1])]
+        for copy in copies:
+            copy.start()
+        for copy in copies:
+            copy.wait()
+
+    return pl.pallas_call(put, out_shape=[jax.ShapeDtypeStruct((TILE, TILE), F32)] * 2, name="put", in_specs=[anywhere] * 2, out_specs=[anywhere] * 2, scratch_shapes=[dma(2)], compiler_params=pltpu.CompilerParams(vmem_limit_bytes=4 * 1024 * 1024))(*outs)
 
 
 def solution(mesh):

time: 32.5 us -> 32.2 us (level)
  no operation moved by 1% of the time
where the time goes in v3:
time: 32.2 us; the launch traced here: 32.1 us
  Pallas kernels  31.5 us (98%)
  between operations  0.64 us (2%)
    pallas_call x1, Pallas kernels, on_device(): pl.pallas_call(body, out_shape=[jax.ShapeDtypeStruct((TILE, TILE), F32)]...  30.7 us
    pallas_call x1, Pallas kernels, on_device(): pl.pallas_call(put, out_shape=[jax.ShapeDtypeStruct((TILE, TILE), F32)] *...  0.81 us

profile of v3, /device:TPU:39, one launch (start us, length us, event | category | flops | bytes accessed | tf_op | source)
XLA Modules:
  0.0 32.1 jit_solution(4297681318725439901)
XLA Ops:
  0.6 30.7 %socs_step.1 = (f32[256,256]{1,0:T(8,128)S(1)}, f32[256,256]{1,0:T(8,128)S(1)}) custom-call(f32[256,256]{1,0:T(8,128)} %mask_h.1, s32[256,256]{1,0:T(8,128)} %target_h.1, f32[2,12,128,128]{3,2,1,0:T(8,128)} %spec_h.1, bf16[2,384,256]{2,1,0:T(8,128)(2,1)} %constant.8.clone.place_h, bf16[2,256,768]{2,1,0:T(8,128)(2,1)} %constant.9.clone.freq_h, ...), custom_call_target="tpu_custom_call" | custom-call | tf_op jit(solution)/shard_map/socs_step/pallas_call | solution.py:425
  31.3 0.8 %put.1 = (f32[256,256]{1,0:T(8,128)}, f32[256,256]{1,0:T(8,128)}) custom-call(f32[256,256]{1,0:T(8,128)S(1)} %get-tuple-element.4.a, f32[256,256]{1,0:T(8,128)S(1)} %get-tuple-element.5.b), custom_call_target="tpu_custom_call" | custom-call | tf_op jit(solution)/shard_map/put/pallas_call | solution.py:444

commit v4 on v3

--- a/solution.py
+++ b/solution.py
@@ -250,17 +250,22 @@
         for k in range(kernels):
             step(k)
 
-    def to_columns(k):
+    def to_columns(first):
         f_re, f_im = w_part[:, :BAND], w_part[:, BAND:]
-        h_re, h_im = spec_v[0, k], spec_v[1, k]
-        prod = jnp.concatenate([f_re * h_re - f_im * h_im, f_re * h_im + f_im * h_re], axis=0)
-        value = rows_by_table(prod, (ffreq_v[0], ffreq_v[1]))
-        re_c, re_s, im_c, im_s = value[:BAND, :HALF], value[:BAND, HALF:], value[BAND:, :HALF], value[BAND:, HALF:]
-        hi, lo = split(jnp.concatenate([re_c - im_s, re_c + im_s, im_c + re_s, im_c - re_s], axis=1))
-        r_stack[k, pl.ds(0, BAND), :] = hi
-        r_stack[k, pl.ds(BAND, BAND), :] = lo
-
-    loop(to_columns)
+        prods = []
+        for k in (first, first + 1):
+            h_re, h_im = spec_v[0, k], spec_v[1, k]
+            prods += [f_re * h_re - f_im * h_im, f_re * h_im + f_im * h_re]
+        both = rows_by_table(jnp.concatenate(prods, axis=0), (ffreq_v[0], ffreq_v[1]))
+        for i in range(2):
+            value = both[i * 2 * BAND : (i + 1) * 2 * BAND]
+            re_c, re_s, im_c, im_s = value[:BAND, :HALF], value[:BAND, HALF:], value[BAND:, :HALF], value[BAND:, HALF:]
+            hi, lo = split(jnp.concatenate([re_c - im_s, re_c + im_s, im_c + re_s, im_c - re_s], axis=1))
+            r_stack[first + i, pl.ds(0, BAND), :] = hi
+            r_stack[first + i, pl.ds(BAND, BAND), :] = lo
+
+    for k in range(0, kernels, 2):
+        to_columns(k)
 
     i_copies = []
     for b in range(2):

time: 32.2 us -> 32.2 us (level)
  no operation moved by 1% of the time
where the time goes in v4:
time: 32.2 us
  Pallas kernels  31.5 us (98%)
  between operations  0.64 us (2%)
    pallas_call x1, Pallas kernels, on_device(): pl.pallas_call(body, out_shape=[jax.ShapeDtypeStruct((TILE, TILE), F32)]...  30.7 us
    pallas_call x1, Pallas kernels, on_device(): pl.pallas_call(put, out_shape=[jax.ShapeDtypeStruct((TILE, TILE), F32)] *...  0.81 us

profile of v4, /device:TPU:39, one launch (start us, length us, event | category | flops | bytes accessed | tf_op | source)
XLA Modules:
  0.0 32.2 jit_solution(16871346565224169632)
XLA Ops:
  0.6 30.7 %socs_step.1 = (f32[256,256]{1,0:T(8,128)S(1)}, f32[256,256]{1,0:T(8,128)S(1)}) custom-call(f32[256,256]{1,0:T(8,128)} %mask_h.1, s32[256,256]{1,0:T(8,128)} %target_h.1, f32[2,12,128,128]{3,2,1,0:T(8,128)} %spec_h.1, bf16[2,384,256]{2,1,0:T(8,128)(2,1)} %constant.8.clone.place_h, bf16[2,256,768]{2,1,0:T(8,128)(2,1)} %constant.9.clone.freq_h, ...), custom_call_target="tpu_custom_call" | custom-call | tf_op jit(solution)/shard_map/socs_step/pallas_call | solution.py:430
  31.4 0.8 %put.1 = (f32[256,256]{1,0:T(8,128)}, f32[256,256]{1,0:T(8,128)}) custom-call(f32[256,256]{1,0:T(8,128)S(1)} %get-tuple-element.4.a, f32[256,256]{1,0:T(8,128)S(1)} %get-tuple-element.5.b), custom_call_target="tpu_custom_call" | custom-call | tf_op jit(solution)/shard_map/put/pallas_call | solution.py:449
